TPU v7x, 128 devices: a whole 4x4x4 slice. The times are simulated.
128 devices in a mesh: ep: 32 (over z, y, core), dp: 4 (over x).
Axes of the slice: x: 4, y: 4, z: 4, core: 2. Of those that a mesh axis runs over, the one named last changes fastest.
Arguments:
- tokens: bfloat16 [2048, 7168], P(('ep', 'dp')), may hold values from -6 to 6
- routes: int32 [2048, 8], P(('ep', 'dp')), may hold values from 0 to 31, all different within a row; in each aligned block of 16 rows (0 to 15, 16 to 31, ...) at most 8 rows name the same one
- route_logits: float32 [2048, 8], P(('ep', 'dp')), may hold values from -6 to 6
- gate_weight: bfloat16 [32, 7168, 2048], P('ep', None, 'dp'), may hold values from -0.0625 to 0.0625
- up_weight: bfloat16 [32, 7168, 2048], P('ep', None, 'dp'), may hold values from -0.0625 to 0.0625
- down_weight: bfloat16 [32, 2048, 7168], P('ep', 'dp'), may hold values from -0.125 to 0.125
Outputs:
- moe_output: bfloat16 [2048, 7168], P(('ep', 'dp'))
- expert_load: float32 [32], P('ep')
Inputs may be any that keep to these rules, and one draw needn't show every extreme that they name: `routes`: each row names 8 different experts. Within the rows of one device (aligned blocks of 16 rows) no expert is named more than 8 times, and in every draw some expert is named exactly 8 times there; every expert is named somewhere.
All inputs are finite; a program needn't handle non-finite values.
Results may differ from a plain program's by a relative error of at most 0.012.
Values may be sent and summed in bfloat16 or wider, within the bound.
No kernel may reach another device: no remote copies, remote signals or barrier semaphores. Data moves between devices by JAX's collectives and lax.ppermute only.
A program may use at most 128 MiB of HBM per device.

v0:
```python
import jax
import jax.numpy as jnp
from jax import lax
from jax.sharding import Mesh
from jax.sharding import PartitionSpec as P

EP = ("ep_0", "ep_1", "ep_2")
EP_DP = ("ep_0", "ep_1", "ep_2", "dp")
ROUTE_SCALE = 2.5
PRECISE = lax.Precision.HIGHEST


def split_up(x, dim, devices):
    before, after = (x.shape[:dim], x.shape[dim + 1 :])
    return jnp.moveaxis(x.reshape(*before, devices, -1, *after), dim, 0)


def laid_out(parts, dim):
    lengths = list(parts.shape[1:])
    lengths[dim] *= parts.shape[0]
    return jnp.moveaxis(parts, 0, dim).reshape(lengths)


def moved_by_axis(parts, axes, order):
    lengths = [lax.axis_size(a) for a in axes]
    parts = parts.reshape(*lengths, *parts.shape[1:])
    for k in order:
        parts = lax.all_to_all(parts, axes[k], split_axis=k, concat_axis=k, tiled=True)
    return parts.reshape(-1, *parts.shape[len(axes) :])


def core_and_chips(x, groups, order, split_dim, concat_dim):
    devices = lax.axis_size(groups[0]) * lax.axis_size(groups[1])
    parts = split_up(x, split_dim, devices)
    return laid_out(moved_by_axis(parts, groups, order), concat_dim)


def sum_at_owner(x, axis, dim):
    devices = lax.axis_size(axis)
    parts = lax.all_to_all(split_up(x, dim, devices), axis, 0, 0, tiled=True)
    return jnp.sum(parts, axis=0)


def sent_to_all(x, axis):
    copies = jnp.broadcast_to(x, (lax.axis_size(axis), *x.shape))
    return lax.all_to_all(copies, axis, split_axis=0, concat_axis=0, tiled=True)


def over_copies(x, axis):
    return sent_to_all(x, axis).sum(axis=0)


def assignment_slots(flat_routes, experts):
    labels = jnp.arange(experts, dtype=jnp.int32)
    onehot = (flat_routes[:, :, None] == labels[None, None, :]).astype(jnp.int32)
    before = jnp.cumsum(onehot, axis=1) - onehot
    return (jnp.sum(before * onehot, axis=2), jnp.sum(onehot, axis=1))


def pack(members, flat_routes, slot_ids, experts, capacity, top_k):
    blocks, per_block = flat_routes.shape
    tok_dev = per_block // top_k
    member = jnp.arange(blocks, dtype=jnp.int32)[:, None]
    target = ((member * experts + flat_routes) * capacity + slot_ids).reshape(-1)
    source = (member * tok_dev + jnp.arange(per_block, dtype=jnp.int32)[None, :] // top_k).reshape(
        -1
    )
    placing = (
        jnp.arange(blocks * experts * capacity, dtype=jnp.int32)[:, None] == target[None, :]
    ).astype(jnp.bfloat16)
    owners = (source[:, None] == jnp.arange(blocks * tok_dev, dtype=jnp.int32)[None, :]).astype(
        jnp.bfloat16
    )
    picker = jnp.dot(placing, owners, preferred_element_type=jnp.float32).astype(jnp.bfloat16)
    filled = jnp.dot(picker, members, preferred_element_type=jnp.float32).astype(jnp.bfloat16)
    return filled.reshape(blocks, experts, capacity, members.shape[1])


def expert_rows(row_block, gate_w, up_w, down_w):
    gate_act = jnp.dot(row_block, gate_w, preferred_element_type=jnp.float32)
    up_act = jnp.dot(row_block, up_w, preferred_element_type=jnp.float32)
    hidden = (jax.nn.silu(gate_act) * up_act).astype(jnp.bfloat16)
    return jnp.dot(hidden, down_w, preferred_element_type=jnp.float32)


def on_device(tokens, routes, route_logits, gate_weight, up_weight, down_weight):
    tok_dev, top_k = routes.shape
    model_width = tokens.shape[1]
    experts = lax.axis_size(EP)
    groups = lax.axis_size("dp")
    capacity = min(tok_dev // 2, 2 * tok_dev * top_k // experts)
    per_block = tok_dev * top_k
    gate_w = gate_weight[0]
    up_w = up_weight[0]
    down_w = down_weight[0]
    own_flat = routes.reshape(1, per_block)
    own_slots, own_counts = assignment_slots(own_flat, experts)
    buffer = pack(tokens, own_flat, own_slots, experts, capacity, top_k)
    received = core_and_chips(buffer, (("ep_0", "ep_1"), "ep_2"), (1, 0), 1, 1)
    partial_value = expert_rows(
        lax.all_gather(received.reshape(-1, model_width), "dp", axis=0, tiled=True),
        gate_w,
        up_w,
        down_w,
    )
    shares = lax.psum_scatter(
        partial_value.astype(jnp.bfloat16), "dp", scatter_dimension=0, tiled=True
    ).astype(jnp.float32)
    returned = lax.all_to_all(
        shares.reshape(experts, capacity, model_width).astype(jnp.bfloat16),
        EP,
        split_axis=0,
        concat_axis=0,
        tiled=True,
    ).astype(jnp.float32)
    affinity = jax.nn.sigmoid(route_logits)
    weights = (ROUTE_SCALE * affinity / jnp.sum(affinity, axis=1, keepdims=True)).reshape(-1)
    own_target = own_flat[0] * capacity + own_slots[0]
    spread = jnp.where(
        own_target[:, None] == jnp.arange(experts * capacity, dtype=jnp.int32)[None, :],
        weights[:, None],
        0.0,
    )
    owners = (
        jnp.arange(tok_dev, dtype=jnp.int32)[:, None]
        == jnp.arange(per_block, dtype=jnp.int32)[None, :] // top_k
    ).astype(jnp.float32)
    combine = jnp.dot(owners, spread, precision=PRECISE)
    moe_output = jnp.dot(
        combine, returned.reshape(experts * capacity, model_width), precision=PRECISE
    ).astype(jnp.bfloat16)
    local_counts = own_counts[0].astype(jnp.float32)
    group_count = sum_at_owner(local_counts, EP, 0)
    expert_count = over_copies(group_count, "dp")
    mean_count = float(tok_dev * groups * top_k)
    expert_load = expert_count / mean_count
    return (moe_output, expert_load)


def solution(mesh):
    finer = Mesh(mesh.devices.reshape(4, 4, 2, mesh.shape["dp"]), ("ep_0", "ep_1", "ep_2", "dp"))
    in_specs = (
        P(EP_DP, None),
        P(EP_DP, None),
        P(EP_DP, None),
        P(EP, None, "dp"),
        P(EP, None, "dp"),
        P(EP, "dp", None),
    )
    out_specs = (P(EP_DP, None), P(EP))
    return jax.shard_map(
        on_device, mesh=finer, in_specs=in_specs, out_specs=out_specs, check_vma=False
    )
```

profile of v0, /device:TPU:0, one launch (start us, length us, event | category | flops | bytes accessed | tf_op | source)
XLA Modules:
  0.0 443.3 jit_solution(7559866327238742268)
XLA Ops:
  7.2 0.0 copy-start
  7.2 0.0 all-gather.2.cloned.1.call-start
  7.2 0.8 copy.22
  8.0 0.1 squeeze_reshape.3
  8.1 0.1 fusion.15
  8.2 0.2 reduce_window_sum.11
  8.4 0.2 fusion.16
  8.6 0.0 copy-done
  8.6 3.2 convolution_convert_fusion.1
  11.8 2.3 copy.24
  14.1 6.7 %all_to_all.27 = bf16[16,2,1,1,8,7168]{5,4,0,3,2,1:T(8,128)(2,1)S(1)} all-to-all(bf16[16,2,1,1,8,7168]{5,4,0,3,2,1:T(8,128)(2,1)S(1)} %copy.24), channel_id=1, replica_groups=mesh['ep_0'=4,'ep_1'=4,'ep_2'=2,'dp'=4] {'ep_2'}, dimensions={1} | all-to-all | bytes 7340032 | tf_op jit(solution)/shard_map/all_to_all | solution.py:28
  20.8 0.3 copy.25
  21.1 53.6 %all_to_all.28 = bf16[16,2,1,1,8,7168]{5,4,1,3,2,0:T(8,128)(2,1)} all-to-all(bf16[16,2,1,1,8,7168]{5,4,1,3,2,0:T(8,128)(2,1)S(1)} %copy.25), channel_id=1, replica_groups=mesh['ep_0'=4,'ep_1'=4,'ep_2'=2,'dp'=4] {'ep_0','ep_1'}, dimensions={0} | all-to-all | bytes 7340032 | tf_op jit(solution)/shard_map/all_to_all | solution.py:28
  74.7 0.0 all-gather.2.cloned.1.call-update
  74.7 0.0 reduce-scatter.2.cloned.1.call-start
  74.7 133.9 %all-gather.2.cloned.1.call-done = bf16[1024,7168]{1,0:T(8,128)(2,1)} async-done(((bf16[256,7168]{1,0:T(8,128)(2,1)}), bf16[1024,7168]{1,0:T(8,128)(2,1)}) %all-gather.2.cloned.1.call-update) | async-done | bytes 14680080 | tf_op jit(solution)/shard_map/all_gather | solution.py:101
  208.6 0.0 copy-start.3
  208.6 0.0 slice-start
  208.7 13.4 %fusion.1 = f32[1024,512]{1,0:T(8,128)S(1)} fusion(bf16[1024,7168]{1,0:T(8,128)(2,1)} %all-gather.2.cloned.1.call-done, bf16[1,7168,512]{2,1,0:T(8,128)(2,1)} %param.10), kind=kOutput, calls=%fused_computation.4 | convolution fusion | flops 7516192768 | bytes 24117248 | tf_op jit(solution)/shard_map/dot_general | solution.py:81
  222.0 0.0 copy-done.3
  222.0 0.0 slice-start.1
  222.0 10.3 %multiply_convert_fusion = bf16[1024,512]{1,0:T(8,128)(2,1)S(1)} fusion(f32[1024,512]{1,0:T(8,128)S(1)} %fusion.1, bf16[1024,7168]{1,0:T(8,128)(2,1)S(1)} %copy-done.3, bf16[1,7168,512]{2,1,0:T(8,128)(2,1)} %param.9), kind=kOutput, calls=%fused_computation.9 | convolution fusion | flops 7519338496 | bytes 25165824 | tf_op jit(solution)/shard_map/dot_general | solution.py:80
  232.3 0.0 slice-done
  232.3 0.0 slice-done.1
  232.3 11.1 %convolution_convert_fusion = bf16[1024,7168]{1,0:T(8,128)(2,1)} fusion(bf16[1024,512]{1,0:T(8,128)(2,1)S(1)} %multiply_convert_fusion, bf16[1,512,7168]{2,1,0:T(8,128)(2,1)S(1)} %bitcast.29), kind=kOutput, calls=%fused_computation | convolution fusion | flops 7523532800 | bytes 23068672 | tf_op jit(solution)/shard_map/dot_general | solution.py:83
  243.4 0.0 reduce-scatter.2.cloned.1.call-update
  243.4 0.0 copy-start.2
  243.4 0.0 copy-start.1
  243.5 0.1 copy.26
  243.5 14.5 %all_to_all.29 = f32[32,1,1]{2,1,0:T(1,128)S(1)} all-to-all(f32[32,1,1]{2,1,0:T(1,128)S(1)} %copy.26), channel_id=1, replica_groups=mesh['ep_0'=4,'ep_1'=4,'ep_2'=2,'dp'=4] {'ep_0','ep_1','ep_2'}, dimensions={0} | all-to-all | bytes 256 | tf_op jit(solution)/shard_map/all_to_all | solution.py:40
  258.1 0.6 reduce_sum.48
  258.7 0.6 broadcast_in_dim.29
  259.4 9.0 %all_to_all.30 = f32[4,1,1]{2,1,0:T(1,128)S(1)} all-to-all(f32[4,1,1]{2,1,0:T(1,128)S(1)} %broadcast_in_dim.29), channel_id=1, replica_groups=mesh['ep_0'=4,'ep_1'=4,'ep_2'=2,'dp'=4] {'dp'}, dimensions={0} | all-to-all | bytes 32 | tf_op jit(solution)/shard_map/all_to_all | solution.py:46
  268.4 107.6 %reduce-scatter.2.cloned.1.call-done = bf16[256,7168]{1,0:T(8,128)(2,1)} async-done(((bf16[1024,7168]{1,0:T(8,128)(2,1)}), bf16[256,7168]{1,0:T(8,128)(2,1)}) %reduce-scatter.2.cloned.1.call-update) | async-done | bytes 3670032 | tf_op jit(solution)/shard_map/reduce_scatter | solution.py:106
  376.0 7.4 %all-to-all-start.2 = ((bf16[32,8,7168]{2,1,0:T(8,128)(2,1)}), bf16[32,8,7168]{2,1,0:T(8,128)(2,1)}, u32[]{:S(2)}, u32[]{:S(2)}) async-start(bf16[32,8,7168]{2,1,0:T(8,128)(2,1)} %bitcast.27), calls=%async_computation.3 | async-start | bytes 7340032 | tf_op jit(solution)/shard_map/all_to_all | solution.py:109
  383.4 0.0 copy-done.2
  383.4 0.1 copy.23
  383.5 0.1 broadcast_in_dim.16
  383.6 0.2 fusion.8
  383.8 0.6 reduce_sum.49
  385.1 45.9 %all-to-all-done.2 = bf16[32,8,7168]{2,1,0:T(8,128)(2,1)} async-done(((bf16[32,8,7168]{2,1,0:T(8,128)(2,1)}), bf16[32,8,7168]{2,1,0:T(8,128)(2,1)}, u32[]{:S(2)}, u32[]{:S(2)}) %all-to-all-start.2) | async-done | bytes 3670048 | tf_op jit(solution)/shard_map/all_to_all | solution.py:109
  431.1 4.3 convolution_convert_fusion.2
  435.3 0.0 copy-done.1
  (6 shorter events, 0.1 us)
Async XLA Ops:
  7.2 1.4 copy-start
  7.2 201.5 %all-gather.2.cloned.1.call-start = ((), (), s32[]{:S(2)}) async-start(), calls=%async_computation.6 | async-start | bytes 18350080 | tf_op jit(solution)/shard_map/all_gather | solution.py:101
  74.7 301.3 %reduce-scatter.2.cloned.1.call-start = ((), (), s32[]{:S(2)}) async-start(), calls=%async_computation.7 | async-start | bytes 18350080 | tf_op jit(solution)/shard_map/reduce_scatter | solution.py:106
  208.6 13.4 %copy-start.3 = (bf16[1024,7168]{1,0:T(8,128)(2,1)S(1)}, bf16[1024,7168]{1,0:T(8,128)(2,1)}, u32[]{:S(2)}) copy-start(bf16[1024,7168]{1,0:T(8,128)(2,1)} %all-gather.2.cloned.1.call-done) | copy-start | bytes 44040196
  208.6 23.7 %slice-start = ((s8[7340032]{0:T(1024)(128)(4,1)}), s8[4194304]{0:T(1024)(128)(4,1)S(1)}, s32[]{:S(2)}) async-start(s8[7340032]{0:T(1024)(128)(4,1)} %bitcast.28), calls=%async_computation.8 | async-start | bytes 8388608
  222.0 10.3 %slice-start.1 = ((s8[7340032]{0:T(1024)(128)(4,1)}), s8[3145728]{0:T(1024)(128)(4,1)S(1)}, s32[]{:S(2)}) async-start(s8[7340032]{0:T(1024)(128)(4,1)} %bitcast.28), calls=%async_computation.9 | async-start | bytes 6291456
  243.4 140.0 %copy-start.2 = (f32[16,8]{0,1:T(8,128)S(1)}, f32[16,8]{0,1:T(8,128)}, u32[]{:S(2)}) copy-start(f32[16,8]{0,1:T(8,128)} %param.8) | copy-start | bytes 1540
  243.4 191.9 %copy-start.1 = (bf16[16,7168]{1,0:T(8,128)(2,1)S(1)}, bf16[16,7168]{1,0:T(8,128)(2,1)}, u32[]{:S(2)}) copy-start(bf16[16,7168]{1,0:T(8,128)(2,1)} %param.6) | copy-start | bytes 688132
  376.0 55.1 %all-to-all-start.2 = ((bf16[32,8,7168]{2,1,0:T(8,128)(2,1)}), bf16[32,8,7168]{2,1,0:T(8,128)(2,1)}, u32[]{:S(2)}, u32[]{:S(2)}) async-start(bf16[32,8,7168]{2,1,0:T(8,128)(2,1)} %bitcast.27), calls=%async_computation.3 | async-start | bytes 7340032 | tf_op jit(solution)/shard_map/all_to_all | solution.py:109
Sparse Core Ops, SparseCore 0:
  74.8 133.7 all-gather.1
  243.5 132.4 reduce-scatter.1
where the time goes:
time: 444 us; the launch traced here: 443 us
  waiting for transfers between devices  288 us (65%)
  blocking collectives  83.8 us (19%)
  matrix products  42.4 us (10%)
  between operations  16 us (4%)
  starting transfers between devices  7.45 us (2%)
    all_gather x1, waiting for transfers between devices, on_device(): lax.all_gather(received.reshape(-1, model_width), 'dp', axis=0, tiled=True)  134 us
    reduce_scatter x1, waiting for transfers between devices, on_device(): lax.psum_scatter(partial_value.astype(jnp.bfloat16), 'dp', scatter_dimens...  108 us
    all_to_all x2, blocking collectives, moved_by_axis(): lax.all_to_all(parts, axes[k], split_axis=k, concat_axis=k, tiled=True)  60.3 us
    all_to_all x1, waiting for transfers between devices, on_device(): lax.all_to_all(shares.reshape(experts, capacity, model_width).astype(jnp....  45.9 us
    all_to_all x1, blocking collectives, sum_at_owner(): parts = lax.all_to_all(split_up(x, dim, devices), axis, 0, 0, tiled=True)  14.5 us
    dot_general x1, matrix products, expert_rows(): up_act = jnp.dot(row_block, up_w, preferred_element_type=jnp.float32)  13.4 us
    dot_general x1, matrix products, expert_rows(): return jnp.dot(hidden, down_w, preferred_element_type=jnp.float32)  11.1 us
    dot_general x1, matrix products, expert_rows(): gate_act = jnp.dot(row_block, gate_w, preferred_element_type=jnp.float32)  10.3 us
  transfers between devices with their start and end apart: 3, of which 3 were waited for; matrix products, arithmetic and copies ran while one was open for 1% of the time, Pallas kernels for 0%

commit v1 on v0

--- a/solution.py
+++ b/solution.py
@@ -8,6 +8,11 @@
 EP_DP = ("ep_0", "ep_1", "ep_2", "dp")
 ROUTE_SCALE = 2.5
 PRECISE = lax.Precision.HIGHEST
+
+
+def tiled_gather(x, axis, dim):
+    copies = jnp.concatenate([x] * lax.axis_size(axis), axis=dim)
+    return lax.all_to_all(copies, axis, dim, dim, tiled=True)
 
 
 def split_up(x, dim, devices):
@@ -98,10 +103,7 @@
     buffer = pack(tokens, own_flat, own_slots, experts, capacity, top_k)
     received = core_and_chips(buffer, (("ep_0", "ep_1"), "ep_2"), (1, 0), 1, 1)
     partial_value = expert_rows(
-        lax.all_gather(received.reshape(-1, model_width), "dp", axis=0, tiled=True),
-        gate_w,
-        up_w,
-        down_w,
+        tiled_gather(received.reshape(-1, model_width), "dp", 0), gate_w, up_w, down_w
     )
     shares = lax.psum_scatter(
         partial_value.astype(jnp.bfloat16), "dp", scatter_dimension=0, tiled=True

time: 444 us -> 470 us (1.059)
  blocking collectives: 83.8 us -> 243 us
  waiting for transfers between devices: 288 us -> 153 us
    all_to_all x0 -> x1, blocking collectives: none -> 164 us  [tiled_gather(): return lax.all_to_all(copies, axis, dim, dim, tiled=True)]
    all_gather x1 -> x0, waiting for transfers between devices: 134 us -> none  [on_device(): lax.all_gather(received.reshape(-1, model_width), 'dp', axis=0, tiled=True)]
  transfers between devices with their start and end apart: 3 -> 2, of which waited for: 3 -> 2; matrix products, arithmetic and copies ran while one was open for 1% -> 1% of each run, Pallas kernels for 0% -> 0%
where the time goes in v1:
time: 470 us; the launch traced here: 469 us
  blocking collectives  243 us (52%)
  waiting for transfers between devices  153 us (33%)
  matrix products  42 us (9%)
  between operations  15.9 us (3%)
  starting transfers between devices  7.4 us (2%)
    all_to_all x1, blocking collectives, tiled_gather(): return lax.all_to_all(copies, axis, dim, dim, tiled=True)  164 us
    reduce_scatter x1, waiting for transfers between devices, on_device(): lax.psum_scatter(partial_value.astype(jnp.bfloat16), 'dp', scatter_dimens...  107 us
    all_to_all x2, blocking collectives, moved_by_axis(): lax.all_to_all(parts, axes[k], split_axis=k, concat_axis=k, tiled=True)  60.2 us
    all_to_all x1, waiting for transfers between devices, on_device(): lax.all_to_all(shares.reshape(experts, capacity, model_width).astype(jnp....  45.9 us
    dot_general x1, matrix products, expert_rows(): return jnp.dot(hidden, down_w, preferred_element_type=jnp.float32)  14.1 us
    all_to_all x1, blocking collectives, sum_at_owner(): parts = lax.all_to_all(split_up(x, dim, devices), axis, 0, 0, tiled=True)  11.5 us
    dot_general x1, matrix products, expert_rows(): up_act = jnp.dot(row_block, up_w, preferred_element_type=jnp.float32)  10.1 us
    dot_general x1, matrix products, expert_rows(): gate_act = jnp.dot(row_block, gate_w, preferred_element_type=jnp.float32)  10.1 us
  transfers between devices with their start and end apart: 2, of which 2 were waited for; matrix products, arithmetic and copies ran while one was open for 1% of the time, Pallas kernels for 0%

profile of v1, /device:TPU:0, one launch (start us, length us, event | category | flops | bytes accessed | tf_op | source)
XLA Modules:
  0.0 469.5 jit_solution(4380244525177039997)
XLA Ops:
  7.2 0.0 copy-start
  7.2 0.0 reduce-scatter.2.cloned.1.call-start
  7.2 0.8 copy.22
  8.0 0.1 squeeze_reshape.3
  8.1 0.1 fusion.15
  8.2 0.2 reduce_window_sum.11
  8.4 0.2 fusion.16
  8.6 0.0 copy-done
  8.6 3.2 convolution_convert_fusion.1
  11.8 2.3 copy.24
  14.1 6.7 %all_to_all.39 = bf16[16,2,1,1,8,7168]{5,4,0,3,2,1:T(8,128)(2,1)S(1)} all-to-all(bf16[16,2,1,1,8,7168]{5,4,0,3,2,1:T(8,128)(2,1)S(1)} %copy.24), channel_id=1, replica_groups=mesh['ep_0'=4,'ep_1'=4,'ep_2'=2,'dp'=4] {'ep_2'}, dimensions={1} | all-to-all | bytes 7340032 | tf_op jit(solution)/shard_map/all_to_all | solution.py:33
  20.8 0.3 copy.25
  21.1 53.5 %all_to_all.40 = bf16[16,2,1,1,8,7168]{5,4,1,3,2,0:T(8,128)(2,1)S(1)} all-to-all(bf16[16,2,1,1,8,7168]{5,4,1,3,2,0:T(8,128)(2,1)S(1)} %copy.25), channel_id=1, replica_groups=mesh['ep_0'=4,'ep_1'=4,'ep_2'=2,'dp'=4] {'ep_0','ep_1'}, dimensions={0} | all-to-all | bytes 7340032 | tf_op jit(solution)/shard_map/all_to_all | solution.py:33
  74.6 1.3 pad_maximum_fusion
  75.8 164.1 %all_to_all.41 = bf16[4,256,7168]{2,1,0:T(8,128)(2,1)S(1)} all-to-all(bf16[4,256,7168]{2,1,0:T(8,128)(2,1)S(1)} %bitcast.27), channel_id=1, replica_groups=mesh['ep_0'=4,'ep_1'=4,'ep_2'=2,'dp'=4] {'dp'}, dimensions={0} | all-to-all | bytes 29360128 | tf_op jit(solution)/shard_map/all_to_all | solution.py:15
  240.0 10.1 %fusion.1 = f32[1024,512]{1,0:T(8,128)S(1)} fusion(bf16[1024,7168]{1,0:T(8,128)(2,1)S(1)} %bitcast.28, bf16[1,7168,512]{2,1,0:T(8,128)(2,1)} %param.10), kind=kOutput, calls=%fused_computation.5 | convolution fusion | flops 7516192768 | bytes 24117248 | tf_op jit(solution)/shard_map/dot_general | solution.py:86
  250.1 10.1 %multiply_convert_fusion = bf16[1024,512]{1,0:T(8,128)(2,1)S(1)} fusion(f32[1024,512]{1,0:T(8,128)S(1)} %fusion.1, bf16[1024,7168]{1,0:T(8,128)(2,1)S(1)} %bitcast.29, bf16[1,7168,512]{2,1,0:T(8,128)(2,1)} %param.9), kind=kOutput, calls=%fused_computation.10 | convolution fusion | flops 7519338496 | bytes 25165824 | tf_op jit(solution)/shard_map/dot_general | solution.py:85
  260.2 14.1 %convolution_convert_fusion = bf16[1024,7168]{1,0:T(8,128)(2,1)} fusion(bf16[1024,512]{1,0:T(8,128)(2,1)S(1)} %multiply_convert_fusion, bf16[1,512,7168]{2,1,0:T(8,128)(2,1)} %param.11), kind=kOutput, calls=%fused_computation.1 | convolution fusion | flops 7523532800 | bytes 23068672 | tf_op jit(solution)/shard_map/dot_general | solution.py:88
  274.3 0.0 reduce-scatter.2.cloned.1.call-update
  274.3 0.0 copy-start.2
  274.3 0.0 copy-start.1
  274.4 0.1 copy.26
  274.5 11.5 %all_to_all.42 = f32[32,1,1]{2,1,0:T(1,128)S(1)} all-to-all(f32[32,1,1]{2,1,0:T(1,128)S(1)} %copy.26), channel_id=1, replica_groups=mesh['ep_0'=4,'ep_1'=4,'ep_2'=2,'dp'=4] {'ep_0','ep_1','ep_2'}, dimensions={0} | all-to-all | bytes 256 | tf_op jit(solution)/shard_map/all_to_all | solution.py:45
  285.9 0.6 reduce_sum.48
  286.6 0.6 broadcast_in_dim.29
  287.2 7.6 %all_to_all.43 = f32[4,1,1]{2,1,0:T(1,128)S(1)} all-to-all(f32[4,1,1]{2,1,0:T(1,128)S(1)} %broadcast_in_dim.29), channel_id=1, replica_groups=mesh['ep_0'=4,'ep_1'=4,'ep_2'=2,'dp'=4] {'dp'}, dimensions={0} | all-to-all | bytes 32 | tf_op jit(solution)/shard_map/all_to_all | solution.py:51
  294.8 107.4 %reduce-scatter.2.cloned.1.call-done = bf16[256,7168]{1,0:T(8,128)(2,1)} async-done(((bf16[1024,7168]{1,0:T(8,128)(2,1)}), bf16[256,7168]{1,0:T(8,128)(2,1)}) %reduce-scatter.2.cloned.1.call-update) | async-done | bytes 3670032 | tf_op jit(solution)/shard_map/reduce_scatter | solution.py:108
  402.2 7.4 %all-to-all-start.3 = ((bf16[32,8,7168]{2,1,0:T(8,128)(2,1)}), bf16[32,8,7168]{2,1,0:T(8,128)(2,1)}, u32[]{:S(2)}, u32[]{:S(2)}) async-start(bf16[32,8,7168]{2,1,0:T(8,128)(2,1)} %bitcast.32), calls=%async_computation.4 | async-start | bytes 7340032 | tf_op jit(solution)/shard_map/all_to_all | solution.py:111
  409.6 0.0 copy-done.2
  409.6 0.1 copy.23
  409.7 0.1 broadcast_in_dim.16
  409.8 0.2 fusion.8
  410.0 0.6 reduce_sum.49
  411.3 45.9 %all-to-all-done.3 = bf16[32,8,7168]{2,1,0:T(8,128)(2,1)} async-done(((bf16[32,8,7168]{2,1,0:T(8,128)(2,1)}), bf16[32,8,7168]{2,1,0:T(8,128)(2,1)}, u32[]{:S(2)}, u32[]{:S(2)}) %all-to-all-start.3) | async-done | bytes 3670048 | tf_op jit(solution)/shard_map/all_to_all | solution.py:111
  457.2 4.3 convolution_convert_fusion.2
  461.5 0.0 copy-done.1
  (5 shorter events, 0.1 us)
Async XLA Ops:
  7.2 1.4 copy-start
  7.2 395.0 %reduce-scatter.2.cloned.1.call-start = ((), (), s32[]{:S(2)}) async-start(), calls=%async_computation.7 | async-start | bytes 18350080 | tf_op jit(solution)/shard_map/reduce_scatter | solution.py:108
  274.3 135.2 %copy-start.2 = (f32[16,8]{0,1:T(8,128)S(1)}, f32[16,8]{0,1:T(8,128)}, u32[]{:S(2)}) copy-start(f32[16,8]{0,1:T(8,128)} %param.8) | copy-start | bytes 1540
  274.3 187.2 %copy-start.1 = (bf16[16,7168]{1,0:T(8,128)(2,1)S(1)}, bf16[16,7168]{1,0:T(8,128)(2,1)}, u32[]{:S(2)}) copy-start(bf16[16,7168]{1,0:T(8,128)(2,1)} %param.6) | copy-start | bytes 688132
  402.2 55.0 %all-to-all-start.3 = ((bf16[32,8,7168]{2,1,0:T(8,128)(2,1)}), bf16[32,8,7168]{2,1,0:T(8,128)(2,1)}, u32[]{:S(2)}, u32[]{:S(2)}) async-start(bf16[32,8,7168]{2,1,0:T(8,128)(2,1)} %bitcast.32), calls=%async_computation.4 | async-start | bytes 7340032 | tf_op jit(solution)/shard_map/all_to_all | solution.py:111
Sparse Core Ops, SparseCore 0:
  274.5 127.6 reduce-scatter.1
